TPU v7x, 32 devices: a whole 2x2x4 slice. The times are simulated.
32 devices in a mesh: tm: 16 (over z, y, core), space: 2 (over x).
Axes of the slice: x: 2, y: 2, z: 4, core: 2. Of those that a mesh axis runs over, the one named last changes fastest.
Arguments:
- u_init: float32 [2, 512, 512], P(None, 'space'), may hold values from -8 to 8
- phase: float32 [512, 512], P('space'), may hold values from 0.005 to 0.05
- absorb: float32 [512, 512], P('space'), may hold values from 0.004 to 0.04
Outputs:
- solution: float32 [2, 16, 512, 512], P(None, 'tm', 'space')
All inputs are finite; a program needn't handle non-finite values.
Results may differ from a plain program's by a relative error of at most 0.0003.
Values sent between devices are 32-bit elements; how exact they have to be, the bound alone decides.
A program may use at most 192 MiB of HBM per device.

v0:
```python
import math

import jax
import jax.numpy as jnp
from jax import lax
from jax.sharding import PartitionSpec as P

NX = 512
NY = 512
TS_DEV = 1
ITERS = 4


tau = 400.0
alpha = 0.4
highest = lax.Precision.HIGHEST


def with_halo(cells, sides, width):
    for axis, dim in sides:
        count = lax.axis_size(axis)
        head = lax.slice_in_dim(cells, 0, width, axis=dim)
        tail = lax.slice_in_dim(cells, cells.shape[dim] - width, cells.shape[dim], axis=dim)
        cells = jnp.concatenate(
            [
                lax.ppermute(tail, axis, [(i, (i + 1) % count) for i in range(count)]),
                cells,
                lax.ppermute(head, axis, [((i + 1) % count, i) for i in range(count)]),
            ],
            axis=dim,
        )
    return cells


def shifted(value, axis, steps):
    count = lax.axis_size(axis)
    leading, last = (max(0, -steps), min(count, count - steps))
    return lax.ppermute(value, axis, [(source, source + steps) for source in range(leading, last)])


def tables(length):
    index = jnp.arange(length, dtype=jnp.int32)
    product = index[:, None] * index[None, :] % length
    angle = product.astype(jnp.float32) * (2.0 * math.pi / length)
    return (jnp.cos(angle), jnp.sin(angle))


def mix(field, cosine, sine, sign, pattern):
    real_part = jnp.einsum(pattern, field[0], cosine, precision=highest) - sign * jnp.einsum(
        pattern, field[1], sine, precision=highest
    )
    imag_part = jnp.einsum(pattern, field[1], cosine, precision=highest) + sign * jnp.einsum(
        pattern, field[0], sine, precision=highest
    )
    return jnp.stack([real_part, imag_part])


def laplacian(field):
    padded = with_halo(field, (("space", 2),), 1)
    return (
        padded[:, :, 2:]
        + padded[:, :, :-2]
        + jnp.roll(field, 1, 3)
        + jnp.roll(field, -1, 3)
        - 4.0 * field
    )


def generator(field, phase, absorb):
    curvature = laplacian(field)
    change_real = -tau * curvature[1] + phase * field[1] - absorb * field[0]
    change_imag = tau * curvature[0] - phase * field[0] - absorb * field[1]
    return jnp.stack([change_real, change_imag])


def operate(field, phase, absorb):
    change = generator(field, phase, absorb)
    ahead = field + 0.5 * change
    behind = field - 0.5 * change
    earlier = shifted(ahead, "tm", 1)
    previous = jnp.concatenate([earlier, ahead[:, :-1]], axis=1)
    return behind - previous


def first_mode(block):
    return lax.axis_index("space") * (block * lax.axis_size("tm")) + lax.axis_index("tm") * block


def least_squares(hessenberg, start):
    matrix = [list(line) for line in hessenberg]
    target = [start] + [jnp.zeros((), jnp.float32) for unused in range(ITERS)]
    cosines = []
    sines = []
    for column in range(ITERS):
        for row in range(column):
            upper = matrix[row][column]
            lower = matrix[row + 1][column]
            matrix[row][column] = cosines[row] * upper + sines[row] * lower
            matrix[row + 1][column] = -sines[row] * upper + cosines[row] * lower
        upper = matrix[column][column]
        lower = matrix[column + 1][column]
        radius = jnp.sqrt(upper * upper + lower * lower)
        cosines.append(upper / radius)
        sines.append(lower / radius)
        matrix[column][column] = radius
        target[column + 1] = -sines[column] * target[column]
        target[column] = cosines[column] * target[column]
    factors = [None] * ITERS
    for row in reversed(range(ITERS)):
        total = target[row]
        for other in range(row + 1, ITERS):
            total = total - matrix[row][other] * factors[other]
        factors[row] = total / matrix[row][row]
    return factors


def shards(u_init, phase, absorb):
    parts_time = lax.axis_size("tm")
    parts_space = lax.axis_size("space")
    steps_all = parts_time * TS_DEV
    block = NY // (parts_time * parts_space)
    row_cosine, row_sine = tables(NX)
    column_cosine, column_sine = tables(NY)
    time_cosine, time_sine = tables(steps_all)
    beta = jnp.float32(alpha) ** (1.0 / steps_all)
    frequency = jnp.arange(steps_all).astype(jnp.float32) * (2.0 * math.pi / steps_all)
    cosine = (beta * jnp.cos(frequency))[None, :, None]
    sine = (beta * jnp.sin(frequency))[None, :, None]
    modes_y = (first_mode(block) + jnp.arange(block, dtype=jnp.int32)).astype(jnp.float32)
    symbol_y = 4.0 * jnp.sin(modes_y * (math.pi / NY)) ** 2
    symbol_x = 4.0 * jnp.sin(jnp.arange(NX).astype(jnp.float32) * (math.pi / NX)) ** 2
    symbol = symbol_y[:, None, None] + symbol_x[None, None, :]
    eigen_real = 1.0 - cosine + tau * symbol * sine / 2.0
    eigen_imag = sine + tau * symbol * (1.0 + cosine) / 2.0
    modulus = eigen_real * eigen_real + eigen_imag * eigen_imag
    ratio_real = eigen_real / modulus
    ratio_imag = eigen_imag / modulus
    step_index = lax.axis_index("tm") * TS_DEV + jnp.arange(TS_DEV, dtype=jnp.int32)
    weights = jnp.float32(alpha) ** (step_index.astype(jnp.float32) / steps_all)
    start_field = u_init[:, None]
    first = start_field + 0.5 * generator(start_field, phase, absorb)
    right_side = jnp.where((step_index == 0)[None, :, None, None], first, 0.0)
    corrected = []
    hessenberg = [
        [jnp.zeros((), jnp.float32) for unused in range(ITERS)] for other in range(ITERS + 1)
    ]
    basis = []
    pending = right_side
    start = None
    for column in range(ITERS):
        weighted = pending * weights[None, :, None, None]
        spread = mix(weighted, column_cosine, column_sine, -1.0, "trc,kc->ktr")
        rows_done = mix(
            lax.all_to_all(spread, "space", split_axis=1, concat_axis=3, tiled=True),
            row_cosine,
            row_sine,
            -1.0,
            "ytr,kr->ytk",
        )
        modes = lax.all_to_all(rows_done, "tm", split_axis=1, concat_axis=2, tiled=True)
        spectrum = mix(modes, time_cosine, time_sine, -1.0, "ytx,kt->ykx")
        solved = jnp.stack(
            [
                spectrum[0] * ratio_real + spectrum[1] * ratio_imag,
                spectrum[1] * ratio_real - spectrum[0] * ratio_imag,
            ]
        )
        timed = mix(solved, time_cosine, time_sine, 1.0, "ykx,tk->ytx") / steps_all
        returned = lax.all_to_all(timed, "tm", split_axis=2, concat_axis=1, tiled=True)
        returned = mix(returned, row_cosine, row_sine, 1.0, "ytk,rk->ytr") / NX
        result = (
            mix(
                lax.all_to_all(returned, "space", split_axis=3, concat_axis=1, tiled=True),
                column_cosine,
                column_sine,
                1.0,
                "ktr,ck->trc",
            )
            / NY
        )
        raw_update = result / weights[None, :, None, None]
        raw_image = operate(raw_update, phase, absorb)
        partial_value = tuple(
            (
                jnp.sum(raw_image * basis[row]) if row < column else jnp.zeros((), jnp.float32)
                for row in range(ITERS - 1)
            )
        )
        totals = lax.psum(
            partial_value + (jnp.sum(raw_image * pending), jnp.sum(pending * pending)),
            ("tm", "space"),
        )
        length = jnp.sqrt(totals[-1])
        if column == 0:
            start = length
        else:
            hessenberg[column][column - 1] = length
        basis.append(pending / length)
        update = raw_update / length
        corrected.append(update)
        image = raw_image / length
        products = [totals[row] / length for row in range(column)]
        products.append(totals[-2] / (length * length))
        for vector, amount in zip(basis, products):
            image = image - amount * vector
        for row in range(column + 1):
            hessenberg[row][column] = products[row]
        pending = image
    hessenberg[ITERS][ITERS - 1] = jnp.sqrt(lax.psum(jnp.sum(pending * pending), ("tm", "space")))
    factors = least_squares(hessenberg, start)
    solution = jnp.zeros_like(right_side)
    for amount, update in zip(factors, corrected):
        solution = solution + amount * update
    return solution


def solution(mesh):
    placed = (P(None, "space", None), P("space", None), P("space", None))
    return jax.shard_map(
        shards, mesh=mesh, in_specs=placed, out_specs=P(None, "tm", "space", None), check_vma=False
    )
```

profile of v0, /device:TPU:0, one launch (start us, length us, event | category | flops | bytes accessed | tf_op | source)
XLA Modules:
  0.0 1159.8 jit_solution(10890085248491660023)
XLA Ops:
  32.1 16.2 %all_to_all.240 = f32[2,512,1,256]{3,2,0,1:T(1,128)S(1)} all-to-all(f32[2,512,1,256]{3,2,0,1:T(1,128)S(1)} %copy.84), channel_id=1, replica_groups=mesh['tm'=16,'space'=2] {'space'}, dimensions={1} | all-to-all | bytes 2097152 | tf_op jit(solution)/shard_map/all_to_all | solution.py:154
  48.7 5.8 convolution_multiply_fusion.13
  54.8 5.9 convolution_multiply_fusion.12
  66.5 6.0 fusion.28
  74.6 6.1 all-to-all-start.1
  81.0 22.6 %all-to-all-done.1 = f32[2,256,1,512]{3,2,0,1:T(1,128)S(1)} async-done(((f32[2,256,1,512]{3,2,0,1:T(1,128)}), f32[2,256,1,512]{3,2,0,1:T(1,128)S(1)}, u32[]{:S(2)}, u32[]{:S(2)}) %all-to-all-start.1) | async-done | bytes 1048608 | tf_op jit(solution)/shard_map/all_to_all | solution.py:160
  111.2 31.7 %all_to_all.241 = f32[2,16,16,512]{3,1,0,2:T(8,128)S(1)} all-to-all(f32[2,16,16,512]{3,1,0,2:T(8,128)S(1)} %copy.91), channel_id=1, replica_groups=mesh['tm'=16,'space'=2] {'tm'}, dimensions={2} | all-to-all | bytes 2097152 | tf_op jit(solution)/shard_map/all_to_all | solution.py:169
  165.6 17.6 %all_to_all.242 = f32[2,256,1,512]{1,2,0,3:T(1,128)S(1)} all-to-all(f32[2,256,1,512]{1,2,0,3:T(1,128)S(1)} %copy.93), channel_id=1, replica_groups=mesh['tm'=16,'space'=2] {'space'}, dimensions={3} | all-to-all | bytes 2097152 | tf_op jit(solution)/shard_map/all_to_all | solution.py:173
  195.5 5.9 fusion.25
  201.3 5.9 fusion.24
  218.1 53.6 %all-reduce.3 = (f32[]{:T(128)}, f32[]{:T(128)}) all-reduce(f32[]{:T(128)} %fusion.92, f32[]{:T(128)} %get-tuple-element.40), channel_id=1, replica_groups=mesh['tm'=16,'space'=2] {'tm','space'}, use_global_device_ids=true, to_apply=%region_1.2 | all-reduce | flops 2 | bytes 16 | tf_op jit(solution)/shard_map/psum | solution.py:189
  295.8 16.7 %all_to_all.243 = f32[2,512,1,256]{3,2,0,1:T(1,128)S(1)} all-to-all(f32[2,512,1,256]{3,2,0,1:T(1,128)S(1)} %copy.100), channel_id=1, replica_groups=mesh['tm'=16,'space'=2] {'space'}, dimensions={1} | all-to-all | bytes 2097152 | tf_op jit(solution)/shard_map/all_to_all | solution.py:154
  313.7 7.4 convolution_multiply_fusion.9
  321.3 5.9 convolution_multiply_fusion.8
  327.2 5.8 fusion.21
  333.0 6.2 fusion.20
  340.4 28.5 %all_to_all.244 = f32[2,256,1,512]{3,2,0,1:T(1,128)S(1)} all-to-all(f32[2,256,1,512]{3,2,0,1:T(1,128)S(1)} %copy.104), channel_id=1, replica_groups=mesh['tm'=16,'space'=2] {'tm'}, dimensions={1} | all-to-all | bytes 2097152 | tf_op jit(solution)/shard_map/all_to_all | solution.py:160
  376.5 29.5 %all_to_all.245 = f32[2,16,16,512]{3,1,0,2:T(8,128)S(1)} all-to-all(f32[2,16,16,512]{3,1,0,2:T(8,128)S(1)} %copy.107), channel_id=1, replica_groups=mesh['tm'=16,'space'=2] {'tm'}, dimensions={2} | all-to-all | bytes 2097152 | tf_op jit(solution)/shard_map/all_to_all | solution.py:169
  429.6 19.0 %all_to_all.246 = f32[2,256,1,512]{1,2,0,3:T(1,128)S(1)} all-to-all(f32[2,256,1,512]{1,2,0,3:T(1,128)} %copy.109), channel_id=1, replica_groups=mesh['tm'=16,'space'=2] {'space'}, dimensions={3} | all-to-all | bytes 2097152 | tf_op jit(solution)/shard_map/all_to_all | solution.py:173
  449.8 7.4 fusion.172
  463.2 5.9 fusion.17
  469.1 5.9 fusion.16
  487.0 53.4 %all-reduce.2 = (f32[]{:T(128)}, f32[]{:T(128)}, f32[]{:T(128)}) all-reduce(f32[]{:T(128)} %get-tuple-element.13, f32[]{:T(128)} %get-tuple-element.14, f32[]{:T(128)} %get-tuple-element.12), channel_id=1, replica_groups=mesh['tm'=16,'space'=2] {'tm','space'}, use_global_device_ids=true, to_apply=%region_9.10 | all-reduce | flops 3 | bytes 24 | tf_op jit(solution)/shard_map/psum | solution.py:189
  564.7 17.0 %all_to_all.247 = f32[2,512,1,256]{3,2,0,1:T(1,128)S(1)} all-to-all(f32[2,512,1,256]{3,2,0,1:T(1,128)S(1)} %copy.118), channel_id=1, replica_groups=mesh['tm'=16,'space'=2] {'space'}, dimensions={1} | all-to-all | bytes 2097152 | tf_op jit(solution)/shard_map/all_to_all | solution.py:154
  584.8 7.4 convolution_multiply_fusion.5
  594.3 6.7 convolution_multiply_fusion.4
  601.0 6.0 fusion.13
  614.1 28.7 %all_to_all.248 = f32[2,256,1,512]{3,2,0,1:T(1,128)S(1)} all-to-all(f32[2,256,1,512]{3,2,0,1:T(1,128)S(1)} %copy.122), channel_id=1, replica_groups=mesh['tm'=16,'space'=2] {'tm'}, dimensions={1} | all-to-all | bytes 2097152 | tf_op jit(solution)/shard_map/all_to_all | solution.py:160
  650.4 29.7 %all_to_all.249 = f32[2,16,16,512]{3,1,0,2:T(8,128)S(1)} all-to-all(f32[2,16,16,512]{3,1,0,2:T(8,128)S(1)} %copy.125), channel_id=1, replica_groups=mesh['tm'=16,'space'=2] {'tm'}, dimensions={2} | all-to-all | bytes 2097152 | tf_op jit(solution)/shard_map/all_to_all | solution.py:169
  706.3 19.0 %all_to_all.250 = f32[2,256,1,512]{1,2,0,3:T(1,128)S(1)} all-to-all(f32[2,256,1,512]{1,2,0,3:T(1,128)} %copy.127), channel_id=1, replica_groups=mesh['tm'=16,'space'=2] {'space'}, dimensions={3} | all-to-all | bytes 2097152 | tf_op jit(solution)/shard_map/all_to_all | solution.py:173
  728.5 7.4 fusion.160
  738.0 6.7 fusion.158
  744.7 6.0 fusion.9
  750.8 5.9 fusion.8
  768.7 53.5 %all-reduce.1 = (f32[]{:T(128)}, f32[]{:T(128)}, f32[]{:T(128)}, f32[]{:T(128)}) all-reduce(f32[]{:T(128)} %get-tuple-element.10, f32[]{:T(128)} %get-tuple-element.11, f32[]{:T(128)} %get-tuple-element.9, f32[]{:T(128)} %get-tuple-element.33), channel_id=1, replica_groups=mesh['tm'=16,'space'=2] {'tm','space'}, use_global_device_ids=true, to_apply=%region_17.18 | all-reduce | flops 4 | bytes 32 | tf_op jit(solution)/shard_map/psum | solution.py:189
  848.4 16.7 %all_to_all.251 = f32[2,512,1,256]{3,2,0,1:T(1,128)S(1)} all-to-all(f32[2,512,1,256]{3,2,0,1:T(1,128)S(1)} %copy.133), channel_id=1, replica_groups=mesh['tm'=16,'space'=2] {'space'}, dimensions={1} | all-to-all | bytes 2097152 | tf_op jit(solution)/shard_map/all_to_all | solution.py:154
  868.3 7.4 convolution_multiply_fusion.1
  877.8 6.7 convolution_multiply_fusion
  884.5 6.0 fusion.5
  897.6 28.8 %all_to_all.252 = f32[2,256,1,512]{3,2,0,1:T(1,128)S(1)} all-to-all(f32[2,256,1,512]{3,2,0,1:T(1,128)S(1)} %copy.137), channel_id=1, replica_groups=mesh['tm'=16,'space'=2] {'tm'}, dimensions={1} | all-to-all | bytes 2097152 | tf_op jit(solution)/shard_map/all_to_all | solution.py:160
  933.9 30.0 %all_to_all.253 = f32[2,16,16,512]{3,1,0,2:T(8,128)S(1)} all-to-all(f32[2,16,16,512]{3,1,0,2:T(8,128)S(1)} %copy.140), channel_id=1, replica_groups=mesh['tm'=16,'space'=2] {'tm'}, dimensions={2} | all-to-all | bytes 2097152 | tf_op jit(solution)/shard_map/all_to_all | solution.py:169
  990.1 18.7 %all_to_all.254 = f32[2,256,1,512]{1,2,0,3:T(1,128)S(1)} all-to-all(f32[2,256,1,512]{1,2,0,3:T(1,128)} %copy.142), channel_id=1, replica_groups=mesh['tm'=16,'space'=2] {'space'}, dimensions={3} | all-to-all | bytes 2097152 | tf_op jit(solution)/shard_map/all_to_all | solution.py:173
  1012.1 7.4 fusion.148
  1021.5 6.7 fusion.146
  1028.2 6.1 fusion.1
  1034.3 5.9 fusion
  1055.5 53.4 %all-reduce = (f32[]{:T(128)}, f32[]{:T(128)}, f32[]{:T(128)}, f32[]{:T(128)}, f32[]{:T(128)}) all-reduce(f32[]{:T(128)} %get-tuple-element.6, f32[]{:T(128)} %get-tuple-element.29, f32[]{:T(128)} %get-tuple-element.8, f32[]{:T(128)} %get-tuple-element.7, f32[]{:T(128)} %get-tuple-element.5), channel_id=1, replica_groups=mesh['tm'=16,'space'=2] {'tm','space'}, use_global_device_ids=true, to_apply=%region_19.20 | all-reduce | flops 5 | bytes 40 | tf_op jit(solution)/shard_map/psum | solution.py:189
  1114.8 40.1 %psum.119 = f32[]{:T(128)} all-reduce(f32[]{:T(128)} %fusion.85), channel_id=1, replica_groups=mesh['tm'=16,'space'=2] {'tm','space'}, use_global_device_ids=true, to_apply=%region_29.30 | all-reduce | flops 1 | bytes 8 | tf_op jit(solution)/shard_map/psum | solution.py:209
  (319 shorter events, 349.8 us)
Async XLA Ops:
  0.8 7.0 collective-permute-start
  3.8 3.1 copy-start
  3.8 4.0 collective-permute-start.1
  7.8 1.9 copy-start.3
  7.8 1.9 copy-start.8
  74.6 29.0 %all-to-all-start.1 = ((f32[2,256,1,512]{3,2,0,1:T(1,128)}), f32[2,256,1,512]{3,2,0,1:T(1,128)S(1)}, u32[]{:S(2)}, u32[]{:S(2)}) async-start(f32[2,256,1,512]{3,2,0,1:T(1,128)} %copy.88), calls=%async_computation.1 | async-start | bytes 2097152 | tf_op jit(solution)/shard_map/all_to_all | solution.py:160
  183.6 5.8 copy-start.27
  195.5 5.9 copy-start.28
  201.3 71.8 %copy-start.1 = (f32[1,1,256,512]{3,2,1,0:T(8,128)}, f32[1,1,256,512]{3,2,1,0:T(8,128)S(1)}, u32[]{:S(2)}) copy-start(f32[1,1,256,512]{3,2,1,0:T(8,128)S(1)} %fusion.25) | copy-start | bytes 1572868
  207.2 65.9 %copy-start.2 = (f32[1,1,256,512]{3,2,1,0:T(8,128)}, f32[1,1,256,512]{3,2,1,0:T(8,128)S(1)}, u32[]{:S(2)}) copy-start(f32[1,1,256,512]{3,2,1,0:T(8,128)S(1)} %fusion.24) | copy-start | bytes 1572868
  207.8 3.7 collective-permute-start.2
  207.8 3.7 collective-permute-start.3
  213.1 3.8 copy-start.22
  213.1 3.8 copy-start.23
  213.4 3.6 collective-permute-start.4
  321.3 5.9 copy-start.39
  327.2 5.9 copy-start.29
  457.3 5.8 copy-start.40
  463.2 5.9 copy-start.30
  469.1 15.6 %copy-start.16 = (f32[1,1,256,512]{3,2,1,0:T(8,128)}, f32[1,1,256,512]{3,2,1,0:T(8,128)S(1)}, u32[]{:S(2)}) copy-start(f32[1,1,256,512]{3,2,1,0:T(8,128)S(1)} %fusion.17) | copy-start | bytes 1572868
  474.9 9.7 copy-start.17
  475.5 3.7 collective-permute-start.5
  475.6 3.7 collective-permute-start.6
  481.1 3.6 collective-permute-start.7
  594.3 6.7 copy-start.35
  594.3 6.7 copy-start.41
  601.0 6.0 copy-start.31
  738.0 6.7 copy-start.36
  738.0 6.7 copy-start.42
  744.7 6.0 copy-start.32
  750.7 15.6 %copy-start.18 = (f32[1,1,256,512]{3,2,1,0:T(8,128)}, f32[1,1,256,512]{3,2,1,0:T(8,128)S(1)}, u32[]{:S(2)}) copy-start(f32[1,1,256,512]{3,2,1,0:T(8,128)S(1)} %fusion.9) | copy-start | bytes 1572868
  756.6 9.7 copy-start.19
  757.2 3.7 collective-permute-start.8
  757.3 3.7 collective-permute-start.9
  762.8 3.6 collective-permute-start.10
  877.8 6.7 copy-start.37
  877.8 6.7 copy-start.43
  884.5 6.1 copy-start.33
  1021.5 6.7 copy-start.38
  1021.5 6.7 copy-start.44
  1028.2 6.1 copy-start.34
  1034.3 11.8 %copy-start.20 = (f32[1,1,256,512]{3,2,1,0:T(8,128)}, f32[1,1,256,512]{3,2,1,0:T(8,128)S(1)}, u32[]{:S(2)}) copy-start(f32[1,1,256,512]{3,2,1,0:T(8,128)S(1)} %fusion.1) | copy-start | bytes 1572868
  1040.2 5.9 copy-start.21
  1040.8 3.7 collective-permute-start.11
  1040.8 3.7 collective-permute-start.12
  1047.4 3.9 collective-permute-start.13
  1050.7 3.5 copy-start.13
  1054.2 1.3 copy-start.15
  (12 other events, 14.0 us)
where the time goes:
time: 1170 us; the launch traced here: 1160 us
  blocking collectives  602 us (51%)
  matrix products  388 us (33%)
  local copies, waits for them, and re-layouts  60.2 us (5%)
  other arithmetic  36.2 us (3%)
  waiting for transfers between devices  35.9 us (3%)
  starting transfers between devices  23.9 us (2%)
  between operations  13.2 us (1%)
    psum x4, blocking collectives, shards(): lax.psum(partial_value + (jnp.sum(raw_image * pending), jnp.sum(pending *...  214 us
    all_to_all x4, blocking collectives, shards(): lax.all_to_all(timed, 'tm', split_axis=2, concat_axis=1, tiled=True)  121 us
    dot_general x24, matrix products, mix(): jnp.einsum(pattern, field[0], cosine, precision=highest)  98.9 us
    dot_general x24, matrix products, mix(): jnp.einsum(pattern, field[1], sine, precision=highest)  98.5 us
    dot_general x24, matrix products, mix(): jnp.einsum(pattern, field[0], sine, precision=highest)  95.7 us
    dot_general x24, matrix products, mix(): jnp.einsum(pattern, field[1], cosine, precision=highest)  95.4 us
    all_to_all x3, blocking collectives, shards(): lax.all_to_all(rows_done, 'tm', split_axis=1, concat_axis=2, tiled=True)  86 us
    all_to_all x4, blocking collectives, shards(): lax.all_to_all(returned, 'space', split_axis=3, concat_axis=1, tiled=True)  74.3 us
  transfers between devices with their start and end apart: 15, of which 13 were waited for; matrix products, arithmetic and copies ran while one was open for 0% of the time, Pallas kernels for 0%

commit v1 on v0

v1 whole, which is shorter than its diff:
```python
import functools
import math

import jax
import jax.numpy as jnp
import numpy as np
from jax import lax
from jax.experimental import pallas as pl
from jax.experimental.pallas import tpu as pltpu
from jax.sharding import PartitionSpec as P

ITERS = 4
tau = 400.0
alpha = 0.4
theta = alpha / (1.0 - alpha)
highest = lax.Precision.HIGHEST
AXES = ("tm", "space")
vmem = pl.BlockSpec(memory_space=pltpu.VMEM)


def with_halo(cells, axis, dim):
    count = lax.axis_size(axis)
    head = lax.slice_in_dim(cells, 0, 1, axis=dim)
    tail = lax.slice_in_dim(cells, cells.shape[dim] - 1, cells.shape[dim], axis=dim)
    return jnp.concatenate(
        [
            lax.ppermute(tail, axis, [(i, (i + 1) % count) for i in range(count)]),
            cells,
            lax.ppermute(head, axis, [((i + 1) % count, i) for i in range(count)]),
        ],
        axis=dim,
    )


def first_side(field, phase, absorb):
    padded = with_halo(field, "space", 1)
    curvature = (
        padded[:, 2:] + padded[:, :-2] + jnp.roll(field, 1, 2) + jnp.roll(field, -1, 2) - 4.0 * field
    )
    change_real = -tau * curvature[1] + phase * field[1] - absorb * field[0]
    change_imag = tau * curvature[0] - phase * field[0] - absorb * field[1]
    return field + 0.5 * jnp.stack([change_real, change_imag])


def tables(length):
    index = np.arange(length)
    angle = (index[:, None] * index[None, :] % length) * (2.0 * math.pi / length)
    return np.cos(angle).astype(np.float32), np.sin(angle).astype(np.float32)


def halves(value):
    high = value.astype(jnp.bfloat16)
    return high, (value - high.astype(jnp.float32)).astype(jnp.bfloat16)


def product(left, right):
    dot = functools.partial(jnp.dot, preferred_element_type=jnp.float32)
    return dot(left[0], right[0]) + (dot(left[0], right[1]) + dot(left[1], right[0]))


def split_kernel(cos_ref, sin_ref, ch_ref, cl_ref, sh_ref, sl_ref):
    ch_ref[...], cl_ref[...] = halves(cos_ref[...])
    sh_ref[...], sl_ref[...] = halves(sin_ref[...])


def grid_kernel(
    steps, got_ref, ch_ref, cl_ref, sh_ref, sl_ref, lc_ref, ls_ref, phase_ref, absorb_ref, z_ref, out_ref
):
    devices, _, block, lanes = got_ref.shape
    size = devices * block
    cosine = (ch_ref[...], cl_ref[...])
    sine = (sh_ref[...], sl_ref[...])
    real = halves(got_ref[:, 0].reshape(size, lanes))
    imag = halves(got_ref[:, 1].reshape(size, lanes))
    mid_real = halves(product(cosine, real) - product(sine, imag))
    mid_imag = halves(product(sine, real) + product(cosine, imag))
    lane_cos, lane_sin = halves(lc_ref[0]), halves(ls_ref[0])
    back_cos, back_sin = halves(lc_ref[1]), halves(ls_ref[1])
    z_real = product(mid_real, back_cos) - product(mid_imag, back_sin)
    z_imag = product(mid_real, back_sin) + product(mid_imag, back_cos)
    z_ref[0] = z_real
    z_ref[1] = z_imag
    late = lax.broadcasted_iota(jnp.int32, (size, lanes), 1) % steps > 0
    sum_real = z_real + jnp.where(late, pltpu.roll(z_real, 1, 1), 0.0)
    sum_imag = z_imag + jnp.where(late, pltpu.roll(z_imag, 1, 1), 0.0)
    phase, absorb = phase_ref[...], absorb_ref[...]
    real = halves(absorb * sum_real - phase * sum_imag)
    imag = halves(absorb * sum_imag + phase * sum_real)
    mid_real = halves(product(real, lane_cos) + product(imag, lane_sin))
    mid_imag = halves(product(imag, lane_cos) - product(real, lane_sin))
    out_ref[:, 0] = (product(cosine, mid_real) + product(sine, mid_imag)).reshape(devices, block, lanes)
    out_ref[:, 1] = (product(cosine, mid_imag) - product(sine, mid_real)).reshape(devices, block, lanes)


def fourier(values, sign):
    count = len(values)
    if count == 1:
        return values
    even = fourier(values[0::2], sign)
    odd = fourier(values[1::2], sign)
    first, second = [], []
    for k in range(count // 2):
        angle = sign * 2.0 * math.pi * k / count
        cosine, sine = math.cos(angle), math.sin(angle)
        real, imag = odd[k]
        if k == 0:
            turned = (real, imag)
        elif 4 * k == count:
            turned = (-imag, real) if sign > 0 else (imag, -real)
        else:
            turned = (cosine * real - sine * imag, cosine * imag + sine * real)
        first.append((even[k][0] + turned[0], even[k][1] + turned[1]))
        second.append((even[k][0] - turned[0], even[k][1] - turned[1]))
    return first + second


def tile_of(block, lanes):
    return min(8, block), min(128, lanes)


def solve_tile(w, coefs, steps, row, lane):
    ratio_real, ratio_imag, scale_real, scale_imag, q = coefs
    wr, wi = w
    zr = wr * scale_real - wi * scale_imag
    zi = wr * scale_imag + wi * scale_real
    width = zr.shape[1]
    when = lax.broadcasted_iota(jnp.int32, zr.shape, 1) % steps

    def wrapped(value, amount):
        back = (amount - steps) % width
        return alpha * (pltpu.roll(value, back, 1) if back else value)

    pr, pi = ratio_real, ratio_imag
    amount = 1
    while amount < steps:
        late = when >= amount
        hr = jnp.where(late, pltpu.roll(zr, amount, 1), wrapped(zr, amount))
        hi = jnp.where(late, pltpu.roll(zi, amount, 1), wrapped(zi, amount))
        zr, zi = zr + pr * hr - pi * hi, zi + pr * hi + pi * hr
        pr, pi = pr * pr - pi * pi, 2.0 * pr * pi
        amount *= 2
    hr, hi = wrapped(zr, 1), wrapped(zi, 1)
    first = when == 0
    xr = jnp.where(first, hr + q * hi, 0.0)
    xi = jnp.where(first, hi - q * hr, 0.0)
    return (zr, zi), (xr - theta * wr, xi - theta * wi)


def mode_kernel(steps, start, last, *refs):
    refs = list(refs)
    got_ref = refs.pop(0)
    carry_ref = None if start else refs.pop(0)
    if last:
        old_refs = [refs.pop(0) for unused in range(ITERS)]
        gram_ref = refs.pop(0)
        devices, block, lanes = got_ref.shape[0], got_ref.shape[2], got_ref.shape[3]
    else:
        coef_refs = [refs.pop(0) for unused in range(5)]
        w_ref = None if start else refs.pop(0)
        next_ref, send_ref = refs
        devices, _, block, lanes = send_ref.shape
    high, wide = tile_of(block, lanes)
    across = lanes // wide
    if last:
        gram_ref[...] = jnp.zeros_like(gram_ref)

    def tile(index, unused):
        row = pl.ds(pl.multiple_of(index // across * high, high), high)
        lane = pl.ds(pl.multiple_of(index % across * wide, wide), wide)
        if start:
            w = [(got_ref[0, k, row, lane], got_ref[1, k, row, lane]) for k in range(devices)]
        else:
            values = [(got_ref[k, 0, row, lane], got_ref[k, 1, row, lane]) for k in range(devices)]
            values = fourier(values, -1)
            w = [
                (values[k][0] + carry_ref[0, k, row, lane], values[k][1] + carry_ref[1, k, row, lane])
                for k in range(devices)
            ]
        if last:
            sums = {}
            for k in range(devices):
                vectors = [(r[0, k, row, lane], r[1, k, row, lane]) for r in old_refs] + [w[k]]
                at = 0
                for i in range(ITERS + 1):
                    for j in range(i + 1):
                        term = vectors[i][0] * vectors[j][0] + vectors[i][1] * vectors[j][1]
                        sums[at] = term if k == 0 else sums[at] + term
                        at += 1
            for at in sums:
                gram_ref[at, 0:high, 0:wide] += sums[at]
            return 0
        solved = []
        for k in range(devices):
            coefs = [ref[k, row, lane] for ref in coef_refs]
            z, carry = solve_tile(w[k], coefs, steps, row, lane)
            if w_ref is not None:
                w_ref[0, k, row, lane] = w[k][0]
                w_ref[1, k, row, lane] = w[k][1]
            next_ref[0, k, row, lane] = carry[0]
            next_ref[1, k, row, lane] = carry[1]
            solved.append(z)
        solved = fourier(solved, 1)
        for k in range(devices):
            send_ref[k, 0, row, lane] = solved[k][0]
            send_ref[k, 1, row, lane] = solved[k][1]
        return 0

    lax.fori_loop(0, (block // high) * across, tile, 0)


def call(kernel, shapes, *args):
    out = [jax.ShapeDtypeStruct(shape, kind) for shape, kind in shapes]
    return pl.pallas_call(
        kernel,
        out_shape=out,
        in_specs=[vmem] * len(args),
        out_specs=[vmem] * len(out),
        compiler_params=pltpu.CompilerParams(vmem_limit_bytes=60 * 1024 * 1024),
    )(*args)


def least_squares(hessenberg, start):
    matrix = [list(line) for line in hessenberg]
    target = [start] + [jnp.zeros((), jnp.float32) for unused in range(ITERS)]
    cosines = []
    sines = []
    for column in range(ITERS):
        for row in range(column):
            upper = matrix[row][column]
            lower = matrix[row + 1][column]
            matrix[row][column] = cosines[row] * upper + sines[row] * lower
            matrix[row + 1][column] = -sines[row] * upper + cosines[row] * lower
        upper = matrix[column][column]
        lower = matrix[column + 1][column]
        radius = jnp.sqrt(upper * upper + lower * lower)
        cosines.append(upper / radius)
        sines.append(lower / radius)
        matrix[column][column] = radius
        target[column + 1] = -sines[column] * target[column]
        target[column] = cosines[column] * target[column]
    factors = [None] * ITERS
    for row in reversed(range(ITERS)):
        total = target[row]
        for other in range(row + 1, ITERS):
            total = total - matrix[row][other] * factors[other]
        factors[row] = total / matrix[row][row]
    return factors


def combination(gram):
    count = ITERS + 1
    entry = lambda i, j: gram[i * (i + 1) // 2 + j] if i >= j else gram[j * (j + 1) // 2 + i]
    norms = [jnp.sqrt(jnp.maximum(entry(i, i), 1e-30)) for i in range(count)]
    factor = [[None] * count for unused in range(count)]
    for j in range(count):
        for i in range(j, count):
            value = entry(i, j) / (norms[i] * norms[j])
            for k in range(j):
                value = value - factor[i][k] * factor[j][k]
            if i == j:
                factor[i][i] = jnp.sqrt(jnp.maximum(value, 1e-10))
            else:
                factor[i][j] = value / factor[j][j]
    zero = jnp.zeros((), jnp.float32)
    upper = [[factor[j][i] * norms[j] if j >= i else zero for j in range(count)] for i in range(count)]
    matrix = [
        [(1.0 + theta) * upper[i][j] + upper[i][j + 1] for j in range(ITERS)] for i in range(count)
    ]
    return least_squares(matrix, norms[0] * factor[0][0])


def exchange(value):
    return lax.all_to_all(value, AXES, split_axis=0, concat_axis=0, tiled=True)


def shards(u_init, phase, absorb):
    steps, spaces = lax.axis_size("tm"), lax.axis_size("space")
    devices = steps * spaces
    columns = u_init.shape[2]
    rows = u_init.shape[1] * spaces
    block = columns // devices
    local = rows // devices
    lanes = local * steps
    inner = local // spaces
    f32 = jnp.float32
    me = lax.axis_index("tm") * spaces + lax.axis_index("space")
    cosine_np, sine_np = tables(columns)
    cosine, sine = jnp.asarray(cosine_np), jnp.asarray(sine_np)
    row_cos_np, row_sin_np = tables(rows)
    half = ((columns, columns), jnp.bfloat16)
    table = call(split_kernel, [half] * 4, cosine, sine)

    first = first_side(u_init, phase, absorb)
    pieces = jnp.concatenate([phase[None], absorb[None]]).reshape(2, inner, devices, columns)
    pieces = lax.dynamic_slice_in_dim(pieces, lax.axis_index("tm") * spaces, spaces, axis=2)
    pieces = lax.all_to_all(pieces, "space", split_axis=2, concat_axis=1, tiled=True)
    pieces = pieces.reshape(2, local, columns)
    spread = np.repeat(np.eye(local, dtype=np.float32), steps, axis=1)
    scale = 0.5 / (rows * columns)
    wide_pieces = jnp.einsum("frq,rl->fql", pieces * scale, jnp.asarray(spread), precision=highest)

    mine = lax.axis_index("tm") * spaces * block
    need_cos = lax.dynamic_slice_in_dim(cosine, mine, spaces * block, axis=0)
    need_sin = lax.dynamic_slice_in_dim(sine, mine, spaces * block, axis=0)
    dot = functools.partial(jnp.einsum, precision=highest)
    column = jnp.stack(
        [
            dot("kq,pq->kp", need_cos, first[0]) + dot("kq,pq->kp", need_sin, first[1]),
            dot("kq,pq->kp", need_cos, first[1]) - dot("kq,pq->kp", need_sin, first[0]),
        ]
    )
    column = lax.all_to_all(column, "space", split_axis=1, concat_axis=2, tiled=True)
    row_cos, row_sin = jnp.asarray(row_cos_np), jnp.asarray(row_sin_np)
    side = jnp.stack(
        [
            dot("kp,pa->ka", column[0], row_cos) + dot("kp,pa->ka", column[1], row_sin),
            dot("kp,pa->ka", column[1], row_cos) - dot("kp,pa->ka", column[0], row_sin),
        ]
    )
    side = side.reshape(2, block, devices, local).transpose(0, 2, 1, 3)
    place = np.zeros((local, lanes), np.float32)
    place[np.arange(local), np.arange(local) * steps] = 1.0
    w = jnp.einsum("cmkr,rl->cmkl", side, jnp.asarray(place), precision=highest)

    lane_index = jnp.arange(lanes) // steps
    mode_x = (lane_index[None, :] + local * jnp.arange(devices)[:, None]).astype(f32)
    mode_y = (me * block + jnp.arange(block)).astype(f32)
    symbol_x = 4.0 * jnp.sin(mode_x * (math.pi / rows)) ** 2
    symbol_y = 4.0 * jnp.sin(mode_y * (math.pi / columns)) ** 2
    q = 0.5 * tau * (symbol_x[:, None, :] + symbol_y[None, :, None])
    below = 1.0 / (1.0 + q * q)
    ratio_real, ratio_imag = (1.0 - q * q) * below, -2.0 * q * below
    pr, pi = ratio_real, ratio_imag
    amount = 1
    while amount < steps:
        pr, pi = pr * pr - pi * pi, 2.0 * pr * pi
        amount *= 2
    dr, di = 1.0 - alpha * pr, -alpha * pi
    dr, di = dr - q * di, di + q * dr
    under = 1.0 / (dr * dr + di * di)
    coefs = (ratio_real, ratio_imag, dr * under, -di * under, q)

    place_of = jnp.arange(lanes)
    at, when = place_of // steps, place_of % steps
    same = (when[:, None] == when[None, :]).astype(f32)
    angle = (at[None, :] * (me + devices * at[:, None])) % rows
    angle = angle.astype(f32) * (2.0 * math.pi / rows)
    lane_cos, lane_sin = jnp.cos(angle) * same, jnp.sin(angle) * same
    lane_cos = jnp.stack([lane_cos, lane_cos.T])
    lane_sin = jnp.stack([lane_sin, lane_sin.T])

    sent = ((devices, 2, block, lanes), f32)
    kept = ((2, devices, block, lanes), f32)
    field = ((2, columns, lanes), f32)
    carry, send = call(functools.partial(mode_kernel, steps, True, False), [kept, sent], w, *coefs)
    basis, updates = [w], []
    for step in range(ITERS):
        z, out = call(
            functools.partial(grid_kernel, steps),
            [field, sent],
            exchange(send),
            *table,
            lane_cos,
            lane_sin,
            wide_pieces[0],
            wide_pieces[1],
        )
        updates.append(z)
        got = exchange(out)
        if step + 1 < ITERS:
            w, carry, send = call(
                functools.partial(mode_kernel, steps, False, False), [kept, kept, sent], got, carry, *coefs
            )
            basis.append(w)
    pairs = (ITERS + 1) * (ITERS + 2) // 2
    (gram,) = call(
        functools.partial(mode_kernel, steps, False, True),
        [((pairs, 8, 128), f32)],
        got,
        carry,
        *basis,
    )
    gram = jnp.sum(gram, axis=(1, 2))
    gram = jnp.sum(exchange(jnp.broadcast_to(gram[None, None], (devices, 1, pairs))), axis=(0, 1))
    factors = combination([gram[i] for i in range(pairs)])
    norm = 1.0 / (rows * columns)
    total = sum((amount * norm) * update for amount, update in zip(factors, updates))
    total = total.reshape(2, columns, spaces, inner, steps).transpose(4, 2, 0, 3, 1)
    total = exchange(total.reshape(devices, 2, inner, columns))
    return total.transpose(1, 2, 0, 3).reshape(2, 1, inner * devices, columns)


def solution(mesh):
    placed = (P(None, "space", None), P("space", None), P("space", None))
    return jax.shard_map(
        shards, mesh=mesh, in_specs=placed, out_specs=P(None, "tm", "space", None), check_vma=False
    )
```

time: 1170 us -> 456 us (0.39)
  matrix products: 388 us -> 7.7 us
  blocking collectives: 602 us -> 249 us
  Pallas kernels: 0 us -> 114 us
  local copies, waits for them, and re-layouts: 60.2 us -> 13.3 us
  other arithmetic: 36.2 us -> 11.3 us
  waiting for transfers between devices: 35.9 us -> 19.9 us
    dot_general x96 -> x10, matrix products: 388 us -> 7.7 us  [the longest x1 1.93 us: shards(): w = jnp.einsum('cmkr,rl->cmkl', side, jnp.asarray(place), precision=highest)]
    psum x5 -> x0, blocking collectives: 254 us -> none  [the longest x4 214 us: shards(): lax.psum(partial_value + (jnp.sum(raw_image * pending), jnp.sum(pending *...]
    pallas_call x0 -> x10, Pallas kernels: none -> 114 us  [call(): pl.pallas_call(kernel, out_shape=out, in_specs=[vmem] * len(args), out_sp...]
    all_to_all x15 -> x9, blocking collectives: 348 us -> 249 us  [exchange(): return lax.all_to_all(value, AXES, split_axis=0, concat_axis=0, tiled=True)]
    slice x43 -> x5, local copies, waits for them, and re-layouts: 31.2 us -> 4.4 us  [the longest x2 2.89 us: first_side(): jnp.roll(field, -1, 2)]
    div x8 -> x0, local copies, waits for them, and re-layouts: 12.6 us -> none  [the longest x4 10.1 us: shards(): returned = mix(returned, row_cosine, row_sine, 1.0, 'ytk,rk->ytr') / NX]
    reduce_sum x8 -> x2, other arithmetic: 13.6 us -> 1.07 us  [the longest x1 1.02 us: shards(): gram = jnp.sum(gram, axis=(1, 2))]
  transfers between devices with their start and end apart: 15 -> 5, of which waited for: 13 -> 2; matrix products, arithmetic and copies ran while one was open for 0% -> 4% of each run, Pallas kernels for 0% -> 4%
where the time goes in v1:
time: 456 us; the launch traced here: 447 us
  blocking collectives  249 us (55%)
  Pallas kernels  114 us (25%)
  waiting for transfers between devices  19.9 us (4%)
  starting transfers between devices  16.7 us (4%)
  between operations  15.1 us (3%)
  local copies, waits for them, and re-layouts  13.3 us (3%)
  other arithmetic  11.3 us (2%)
  matrix products  7.7 us (2%)
    all_to_all x9, blocking collectives, exchange(): return lax.all_to_all(value, AXES, split_axis=0, concat_axis=0, tiled=True)  249 us
    pallas_call x10, Pallas kernels, call(): pl.pallas_call(kernel, out_shape=out, in_specs=[vmem] * len(args), out_sp...  114 us
    all_to_all x1, waiting for transfers between devices, exchange(): return lax.all_to_all(value, AXES, split_axis=0, concat_axis=0, tiled=True)  16.4 us
  transfers between devices with their start and end apart: 5, of which 2 were waited for; matrix products, arithmetic and copies ran while one was open for 4% of the time, Pallas kernels for 4%

profile of v1, /device:TPU:0, one launch (start us, length us, event | category | flops | bytes accessed | tf_op | source)
XLA Modules:
  0.0 446.8 jit_solution(16235885228771321994)
XLA Ops:
  0.0 0.8 fusion.51
  0.8 3.0 collective-permute-start
  3.9 2.1 fusion.49
  6.2 2.0 add_multiply_fusion.1
  8.3 0.8 fusion.50
  9.1 1.6 fusion.5
  11.4 1.0 copy-done.1
  14.8 0.7 copy.64
  15.5 3.3 all-to-all-start
  18.8 0.6 copy.68
  19.4 3.4 all-to-all-done
  22.9 3.3 all-to-all-start.2
  26.3 0.6 fusion.55
  27.5 0.6 convolution_subtract_fusion
  28.1 0.6 convolution_add_fusion
  29.9 1.9 fusion.25.refs_0_.refs_2_
  31.8 17.0 %shard_map.91 = (f32[2,32,16,256]{3,2,1,0:T(8,128)}, f32[32,2,16,256]{3,2,1,0:T(8,128)}) custom-call(f32[2,32,16,256]{3,2,1,0:T(8,128)} %fusion.25.refs_0_.refs_2_, f32[32,16,256]{2,1,0:T(8,128)} %get-tuple-element.67.refs_1_.refs_2_, f32[32,16,256]{2,1,0:T(8,128)} %get-tuple-element.64.refs_2_.refs_3_, f32[32,16,256]{2,1,0:T(8,128)} %get-tuple-element.65.refs_3_.refs_4_, ...), custom_call_target="tpu_custom_call" | custom-call | tf_op jit(solution)/shard_map/pallas_call | solution.py:213
  48.8 7.0 %all-to-all-start.1 = ((f32[32,2,16,256]{3,2,1,0:T(8,128)}), f32[32,2,16,256]{3,2,1,0:T(8,128)S(1)}, u32[]{:S(2)}, u32[]{:S(2)}) async-start(f32[32,2,16,256]{3,2,1,0:T(8,128)} %get-tuple-element.28), calls=%async_computation.1 | async-start | bytes 2097152 | tf_op jit(solution)/shard_map/all_to_all | solution.py:273
  55.8 3.0 shard_map.92
  58.8 2.2 compare_select_fusion.2
  61.0 0.8 pad_maximum_fusion.3.ls_ref
  61.8 0.9 pad_maximum_fusion.2.lc_ref
  62.8 0.7 copy-done.10
  63.5 1.0 fusion.56
  64.5 1.1 slice_bitcast_fusion
  65.6 16.4 %all-to-all-done.1.got_ref = f32[32,2,16,256]{3,2,1,0:T(8,128)S(1)} async-done(((f32[32,2,16,256]{3,2,1,0:T(8,128)}), f32[32,2,16,256]{3,2,1,0:T(8,128)S(1)}, u32[]{:S(2)}, u32[]{:S(2)}) %all-to-all-start.1) | async-done | bytes 1048608 | tf_op jit(solution)/shard_map/all_to_all | solution.py:273
  82.0 1.0 copy-done.3
  83.0 10.0 %shard_map.93 = (f32[2,512,256]{2,1,0:T(8,128)}, f32[32,2,16,256]{3,2,1,0:T(8,128)}) custom-call(f32[32,2,16,256]{3,2,1,0:T(8,128)} %copy-done.3, bf16[512,512]{1,0:T(8,128)(2,1)} %get-tuple-element.29.ch_ref, bf16[512,512]{1,0:T(8,128)(2,1)} %get-tuple-element.30.cl_ref, bf16[512,512]{1,0:T(8,128)(2,1)} %get-tuple-element.31.sh_ref, ...), custom_call_target="tpu_custom_call" | custom-call | tf_op jit(solution)/shard_map/pallas_call | solution.py:213
  92.9 29.9 %all_to_all.74.refs_0_ = f32[32,2,16,256]{3,2,1,0:T(8,128)} all-to-all(f32[32,2,16,256]{3,2,1,0:T(8,128)} %get-tuple-element.33), channel_id=1, replica_groups=mesh['tm'=16,'space'=2] {'tm','space'}, dimensions={0} | all-to-all | bytes 2097152 | tf_op jit(solution)/shard_map/all_to_all | solution.py:273
  122.9 16.0 %shard_map.94 = (f32[2,32,16,256]{3,2,1,0:T(8,128)}, f32[2,32,16,256]{3,2,1,0:T(8,128)}, f32[32,2,16,256]{3,2,1,0:T(8,128)}) custom-call(f32[32,2,16,256]{3,2,1,0:T(8,128)} %all_to_all.74.refs_0_, f32[2,32,16,256]{3,2,1,0:T(8,128)} %get-tuple-element.34.refs_1_, f32[32,16,256]{2,1,0:T(8,128)} %get-tuple-element.67.refs_1_.refs_2_, ...), custom_call_target="tpu_custom_call" | custom-call | tf_op jit(solution)/shard_map/pallas_call | solution.py:213
  138.9 30.1 %all_to_all.75.got_ref = f32[32,2,16,256]{3,2,1,0:T(8,128)} all-to-all(f32[32,2,16,256]{3,2,1,0:T(8,128)} %get-tuple-element.35), channel_id=1, replica_groups=mesh['tm'=16,'space'=2] {'tm','space'}, dimensions={0} | all-to-all | bytes 2097152 | tf_op jit(solution)/shard_map/all_to_all | solution.py:273
  169.1 10.0 %shard_map.95 = (f32[2,512,256]{2,1,0:T(8,128)}, f32[32,2,16,256]{3,2,1,0:T(8,128)}) custom-call(f32[32,2,16,256]{3,2,1,0:T(8,128)} %all_to_all.75.got_ref, bf16[512,512]{1,0:T(8,128)(2,1)} %get-tuple-element.29.ch_ref, bf16[512,512]{1,0:T(8,128)(2,1)} %get-tuple-element.30.cl_ref, bf16[512,512]{1,0:T(8,128)(2,1)} %get-tuple-element.31.sh_ref, ...), custom_call_target="tpu_custom_call" | custom-call | tf_op jit(solution)/shard_map/pallas_call | solution.py:213
  179.1 30.0 %all_to_all.76.refs_0_ = f32[32,2,16,256]{3,2,1,0:T(8,128)} all-to-all(f32[32,2,16,256]{3,2,1,0:T(8,128)} %get-tuple-element.36), channel_id=1, replica_groups=mesh['tm'=16,'space'=2] {'tm','space'}, dimensions={0} | all-to-all | bytes 2097152 | tf_op jit(solution)/shard_map/all_to_all | solution.py:273
  209.0 16.1 %shard_map.96 = (f32[2,32,16,256]{3,2,1,0:T(8,128)}, f32[2,32,16,256]{3,2,1,0:T(8,128)}, f32[32,2,16,256]{3,2,1,0:T(8,128)}) custom-call(f32[32,2,16,256]{3,2,1,0:T(8,128)} %all_to_all.76.refs_0_, f32[2,32,16,256]{3,2,1,0:T(8,128)} %get-tuple-element.37.refs_1_, f32[32,16,256]{2,1,0:T(8,128)} %get-tuple-element.67.refs_1_.refs_2_, ...), custom_call_target="tpu_custom_call" | custom-call | tf_op jit(solution)/shard_map/pallas_call | solution.py:213
  225.1 29.9 %all_to_all.77.got_ref = f32[32,2,16,256]{3,2,1,0:T(8,128)} all-to-all(f32[32,2,16,256]{3,2,1,0:T(8,128)} %get-tuple-element.38), channel_id=1, replica_groups=mesh['tm'=16,'space'=2] {'tm','space'}, dimensions={0} | all-to-all | bytes 2097152 | tf_op jit(solution)/shard_map/all_to_all | solution.py:273
  255.1 10.1 %shard_map.97 = (f32[2,512,256]{2,1,0:T(8,128)}, f32[32,2,16,256]{3,2,1,0:T(8,128)}) custom-call(f32[32,2,16,256]{3,2,1,0:T(8,128)} %all_to_all.77.got_ref, bf16[512,512]{1,0:T(8,128)(2,1)} %get-tuple-element.29.ch_ref, bf16[512,512]{1,0:T(8,128)(2,1)} %get-tuple-element.30.cl_ref, bf16[512,512]{1,0:T(8,128)(2,1)} %get-tuple-element.31.sh_ref, ...), custom_call_target="tpu_custom_call" | custom-call | tf_op jit(solution)/shard_map/pallas_call | solution.py:213
  265.2 29.9 %all_to_all.78.refs_0_ = f32[32,2,16,256]{3,2,1,0:T(8,128)} all-to-all(f32[32,2,16,256]{3,2,1,0:T(8,128)} %get-tuple-element.39), channel_id=1, replica_groups=mesh['tm'=16,'space'=2] {'tm','space'}, dimensions={0} | all-to-all | bytes 2097152 | tf_op jit(solution)/shard_map/all_to_all | solution.py:273
  295.1 16.1 %shard_map.98 = (f32[2,32,16,256]{3,2,1,0:T(8,128)}, f32[2,32,16,256]{3,2,1,0:T(8,128)}, f32[32,2,16,256]{3,2,1,0:T(8,128)}) custom-call(f32[32,2,16,256]{3,2,1,0:T(8,128)} %all_to_all.78.refs_0_, f32[2,32,16,256]{3,2,1,0:T(8,128)} %get-tuple-element.40.refs_1_, f32[32,16,256]{2,1,0:T(8,128)} %get-tuple-element.67.refs_1_.refs_2_, ...), custom_call_target="tpu_custom_call" | custom-call | tf_op jit(solution)/shard_map/pallas_call | solution.py:213
  311.2 30.2 %all_to_all.79.got_ref = f32[32,2,16,256]{3,2,1,0:T(8,128)} all-to-all(f32[32,2,16,256]{3,2,1,0:T(8,128)} %get-tuple-element.41), channel_id=1, replica_groups=mesh['tm'=16,'space'=2] {'tm','space'}, dimensions={0} | all-to-all | bytes 2097152 | tf_op jit(solution)/shard_map/all_to_all | solution.py:273
  341.4 10.0 %shard_map.99 = (f32[2,512,256]{2,1,0:T(8,128)}, f32[32,2,16,256]{3,2,1,0:T(8,128)}) custom-call(f32[32,2,16,256]{3,2,1,0:T(8,128)} %all_to_all.79.got_ref, bf16[512,512]{1,0:T(8,128)(2,1)} %get-tuple-element.29.ch_ref, bf16[512,512]{1,0:T(8,128)(2,1)} %get-tuple-element.30.cl_ref, bf16[512,512]{1,0:T(8,128)(2,1)} %get-tuple-element.31.sh_ref, ...), custom_call_target="tpu_custom_call" | custom-call | tf_op jit(solution)/shard_map/pallas_call | solution.py:213
  351.4 29.9 %all_to_all.80.refs_0_ = f32[32,2,16,256]{3,2,1,0:T(8,128)} all-to-all(f32[32,2,16,256]{3,2,1,0:T(8,128)} %get-tuple-element.42), channel_id=1, replica_groups=mesh['tm'=16,'space'=2] {'tm','space'}, dimensions={0} | all-to-all | bytes 2097152 | tf_op jit(solution)/shard_map/all_to_all | solution.py:273
  381.3 6.0 %shard_map.100 = f32[15,8,128]{2,1,0:T(8,128)} custom-call(f32[32,2,16,256]{3,2,1,0:T(8,128)} %all_to_all.80.refs_0_, f32[2,32,16,256]{3,2,1,0:T(8,128)} %get-tuple-element.43.refs_1_, f32[2,32,16,256]{3,2,1,0:T(8,128)} %fusion.25.refs_0_.refs_2_, f32[2,32,16,256]{3,2,1,0:T(8,128)} %get-tuple-element.44.refs_3_, ...), custom_call_target="tpu_custom_call" | custom-call | tf_op jit(solution)/shard_map/pallas_call | solution.py:213
  387.3 1.0 reduce_sum.18
  388.3 10.7 %all_to_all.81 = f32[32,1,15]{2,1,0:T(1,128)S(1)} all-to-all(f32[32,1,15]{2,1,0:T(1,128)S(1)} %broadcast_in_dim.2), channel_id=1, replica_groups=mesh['tm'=16,'space'=2] {'tm','space'}, dimensions={0} | all-to-all | bytes 3840 | tf_op jit(solution)/shard_map/all_to_all | solution.py:273
  399.1 0.7 fusion.53
  414.1 1.8 multiply_add_fusion
  416.9 27.9 %all_to_all.82 = f32[32,2,8,512]{3,2,1,0:T(8,128)S(1)} all-to-all(f32[32,2,8,512]{3,2,1,0:T(8,128)S(1)} %bitcast.104), channel_id=1, replica_groups=mesh['tm'=16,'space'=2] {'tm','space'}, dimensions={0} | all-to-all | bytes 2097152 | tf_op jit(solution)/shard_map/all_to_all | solution.py:273
  444.8 1.6 copy.73
  (54 shorter events, 6.3 us)
Async XLA Ops:
  0.8 8.3 %collective-permute-start = (f32[2,1,512]{2,1,0:T(1,128)S(1)}, f32[2,1,512]{2,1,0:T(1,128)S(1)}, u32[]{:S(2)}, u32[]{:S(2)}) collective-permute-start(f32[2,1,512]{2,1,0:T(1,128)S(1)} %get-tuple-element.59), channel_id=1, source_target_pairs={{1,0},{0,1},{3,2},{2,3},{5,4},{4,5},{7,6},{6,7},{9,8},{8,9},{11,10... | collective-permute-start | bytes 12296 | tf_op jit(solution)/shard_map/ppermute | solution.py:29
  3.8 5.3 %collective-permute-start.1 = (f32[2,1,512]{2,1,0:T(1,128)S(1)}, f32[2,1,512]{2,1,0:T(1,128)S(1)}, u32[]{:S(2)}, u32[]{:S(2)}) collective-permute-start(f32[2,1,512]{2,1,0:T(1,128)S(1)} %get-tuple-element.60), channel_id=1, source_target_pairs={{0,1},{1,0},{2,3},{3,2},{4,5},{5,4},{6,7},{7,6},{8,9},{9,8},{10,11... | collective-permute-start | bytes 12296 | tf_op jit(solution)/shard_map/ppermute | solution.py:27
  6.2 2.1 copy-start
  9.1 1.6 copy-start.4
  9.1 1.6 copy-start.6
  11.1 1.2 copy-start.1
  12.3 1.2 copy-start.2
  14.2 4.6 %copy-start.5 = (f32[256,512]{1,0:T(8,128)S(1)}, f32[256,512]{1,0:T(8,128)}, u32[]{:S(2)}) copy-start(f32[256,512]{1,0:T(8,128)} %param.11) | copy-start | bytes 1572868
  14.2 4.6 %copy-start.7 = (f32[256,512]{1,0:T(8,128)S(1)}, f32[256,512]{1,0:T(8,128)}, u32[]{:S(2)}) copy-start(f32[256,512]{1,0:T(8,128)} %param.10) | copy-start | bytes 1572868
  15.5 7.4 %all-to-all-start = ((f32[2,32,256]{2,0,1:T(2,128)}), f32[2,32,256]{2,0,1:T(2,128)S(1)}, u32[]{:S(2)}, u32[]{:S(2)}) async-start(f32[2,32,256]{2,0,1:T(2,128)} %copy.64), calls=%async_computation | async-start | bytes 131072 | tf_op jit(solution)/shard_map/all_to_all | solution.py:312
  22.9 25.9 %all-to-all-start.2 = ((f32[2,8,2,512]{3,1,0,2:T(8,128)}), f32[2,8,2,512]{3,1,0,2:T(8,128)S(1)}, u32[]{:S(2)}, u32[]{:S(2)}) async-start(f32[2,8,2,512]{3,1,0,2:T(8,128)} %copy.68), calls=%async_computation.2 | async-start | bytes 131072 | tf_op jit(solution)/shard_map/all_to_all | solution.py:296
  29.2 0.7 copy-start.11
  48.8 33.2 %all-to-all-start.1 = ((f32[32,2,16,256]{3,2,1,0:T(8,128)}), f32[32,2,16,256]{3,2,1,0:T(8,128)S(1)}, u32[]{:S(2)}, u32[]{:S(2)}) async-start(f32[32,2,16,256]{3,2,1,0:T(8,128)} %get-tuple-element.28), calls=%async_computation.1 | async-start | bytes 2097152 | tf_op jit(solution)/shard_map/all_to_all | solution.py:273
  62.8 0.7 copy-start.10
  82.0 1.0 copy-start.3
  381.3 32.8 %copy-start.8 = (f32[2,512,256]{2,1,0:T(8,128)S(1)}, f32[2,512,256]{2,1,0:T(8,128)}, u32[]{:S(2)}) copy-start(f32[2,512,256]{2,1,0:T(8,128)} %get-tuple-element.47) | copy-start | bytes 3145732
  381.3 32.8 %copy-start.9 = (f32[2,512,256]{2,1,0:T(8,128)S(1)}, f32[2,512,256]{2,1,0:T(8,128)}, u32[]{:S(2)}) copy-start(f32[2,512,256]{2,1,0:T(8,128)} %get-tuple-element.48) | copy-start | bytes 3145732
